TPU v7x, 32 devices: a whole 2x2x4 slice. The times are simulated.
32 devices in a mesh: rows: 8 (over y, x, core), cols: 4 (over z).
Axes of the slice: x: 2, y: 2, z: 4, core: 2. Of those that a mesh axis runs over, the one named last changes fastest.
Arguments:
- block_values: bfloat16 [16384, 128], P(('rows', 'cols')), may hold values from -6 to 6
- block_length: int32 [16384], P(('rows', 'cols')), may hold values from 1 to 128
- block_owner: int32 [16384], P(('rows', 'cols')), may hold values from 0 to 4095, as said below
- block_second: int32 [16384], P(('rows', 'cols')), may hold values from 0 to 4095, as said below
- block_third: int32 [16384, 128], P(('rows', 'cols')), may hold values from 0 to 8191
- live_blocks: int32 [32], P(('rows', 'cols')), may hold values from 1 to 512, as said below
- second_factor: bfloat16 [4096, 256], P('cols', 'rows')
- third_factor: bfloat16 [8192, 256], P('cols', 'rows'), may hold values from -6 to 6
Outputs:
- first_factor: float32 [4096, 256], P('cols', 'rows')
Inputs may be any that keep to these rules, and one draw needn't show every extreme that they name: `block_owner`: slot b lies on device d = b // 512 with index r along rows; its row lies in r * 4096 // 8 up to (r + 1) * 4096 // 8 - 1, the device's mode-1 slab. `block_second`: slot b lies on device d = b // 512 with index c along cols; its row lies in c * 4096 // 4 up to (c + 1) * 4096 // 4 - 1. `live_blocks`: some device uses all 512 slots in every draw.
All inputs are finite; a program needn't handle non-finite values.
Results may differ from a plain program's by a relative error of at most 0.0003.
Values may be sent and summed in bfloat16 or wider, within the bound.
A program may use at most 128 MiB of HBM per device.

v0:
```python
import jax
import jax.numpy as jnp
from jax import lax
from jax.sharding import PartitionSpec as P

I_DEV = 128


def gram_product(left, right):
    contract = (((0,), (0,)), ((), ()))
    return lax.dot_general(left, right, contract, preferred_element_type=jnp.float32)


def block_fold(values, third, table):
    group = values.shape[0]
    width = values.shape[1]
    picked = table[third.reshape(group * width)]
    scaled = values.reshape(group * width, 1).astype(jnp.float32) * picked.astype(jnp.float32)
    return jnp.sum(scaled.reshape(group, width, picked.shape[1]), axis=1)


def per_device(
    block_values,
    block_length,
    block_owner,
    block_second,
    block_third,
    live_blocks,
    second_factor,
    third_factor,
):
    n_rows = lax.axis_size("rows")
    n_cols = lax.axis_size("cols")
    row_at = lax.axis_index("rows")
    col_at = lax.axis_index("cols")
    contract = (((0,), (0,)), ((), ()))
    width = block_values.shape[1]
    lane = jnp.arange(width, dtype=jnp.int32)
    slab = I_DEV * n_cols
    owned = jnp.arange(slab, dtype=jnp.int32)
    second_range = lax.all_gather(second_factor, "rows", axis=1, tiled=True)
    third_part = lax.all_gather(third_factor, "cols", axis=0, tiled=True)
    third_whole = lax.all_gather(third_part, "rows", axis=1, tiled=True)
    range_rows = second_range.shape[0]
    local_gram = gram_product(second_range, second_range)
    gram_second = lax.psum(local_gram, "cols") / (range_rows * n_cols)
    gram_third = gram_product(third_whole, third_whole) / third_whole.shape[0]
    gram = gram_second * gram_third
    nblk = block_values.shape[0]
    group = min(nblk, 128)
    count = live_blocks[0]

    def accumulate(step, total):
        start = step * group
        values = lax.dynamic_slice_in_dim(block_values, start, group, 0)
        lengths = lax.dynamic_slice_in_dim(block_length, start, group, 0)
        third = lax.dynamic_slice_in_dim(block_third, start, group, 0)
        second = lax.dynamic_slice_in_dim(block_second, start, group, 0)
        owner = lax.dynamic_slice_in_dim(block_owner, start, group, 0)
        slot = start + jnp.arange(group, dtype=jnp.int32)
        live = (lane[None, :] < lengths[:, None]) & (slot < count)[:, None]
        values = jnp.where(live, values, jnp.zeros((), jnp.bfloat16))
        fold = block_fold(values, third, third_whole)
        contrib = second_range[second - col_at * range_rows].astype(jnp.float32) * fold
        onehot = ((owner - row_at * slab)[:, None] == owned[None, :]).astype(jnp.float32)
        return total + lax.dot_general(
            onehot,
            contrib,
            contract,
            precision=lax.Precision.HIGHEST,
            preferred_element_type=jnp.float32,
        )

    start_total = jnp.zeros((slab, gram.shape[0]), jnp.float32)
    partial_rows = lax.fori_loop(0, (count + group - 1) // group, accumulate, start_total)
    mine = lax.psum_scatter(partial_rows, "cols", scatter_dimension=0, tiled=True)
    factor = jnp.linalg.cholesky(gram)
    solved = jax.scipy.linalg.cho_solve((factor, True), mine.T).T
    moved = lax.all_to_all(
        lax.all_to_all(solved, "rows", split_axis=1, concat_axis=0, tiled=True),
        "cols",
        split_axis=0,
        concat_axis=0,
        tiled=True,
    )
    share = n_rows // n_cols
    owned_rows = mine.shape[0]
    reordered = moved.reshape(n_cols, share, owned_rows, moved.shape[1]).transpose(1, 0, 2, 3)
    return reordered.reshape(n_rows * owned_rows, moved.shape[1])


def solution(mesh):
    return jax.shard_map(
        per_device,
        mesh=mesh,
        in_specs=(
            P(("rows", "cols"), None),
            P(("rows", "cols")),
            P(("rows", "cols")),
            P(("rows", "cols")),
            P(("rows", "cols"), None),
            P(("rows", "cols")),
            P("cols", "rows"),
            P("cols", "rows"),
        ),
        out_specs=P("cols", "rows"),
        check_vma=False,
    )
```

profile of v0, /device:TPU:0, one launch (start us, length us, event | category | flops | bytes accessed | tf_op | source)
XLA Modules:
  0.0 476.4 jit_solution(10479192141841204088)
XLA Ops:
  7.4 11.6 %all_gather.9 = bf16[1024,256]{0,1:T(8,128)(2,1)S(1)} all-gather(bf16[1024,32]{0,1:T(8,128)(2,1)} %param.16), channel_id=1, replica_groups=mesh['rows'=8,'cols'=4] {'rows'}, dimensions={1}, use_global_device_ids=true | all-gather | bytes 589824 | tf_op jit(solution)/shard_map/all_gather | solution.py:41
  19.0 1.1 fusion.24
  20.1 20.9 %all_gather.10 = bf16[8192,32]{0,1:T(8,128)(2,1)} all-gather(bf16[2048,32]{0,1:T(8,128)(2,1)} %param.17), channel_id=1, replica_groups=mesh['rows'=8,'cols'=4] {'cols'}, dimensions={0}, use_global_device_ids=true | all-gather | bytes 655360 | tf_op jit(solution)/shard_map/all_gather | solution.py:42
  41.7 0.2 copy.33
  42.0 15.7 %all-reduce.3.cloned.1.call-done = f32[256,256]{0,1:T(8,128)} async-done(((f32[256,256]{0,1:T(8,128)}), f32[256,256]{0,1:T(8,128)}) %all-reduce.3.cloned.1.call-update) | async-done | bytes 262160 | tf_op jit(solution)/shard_map/psum | solution.py:46
  57.7 18.4 %all-gather.2.cloned.1.call-done = bf16[8192,256]{0,1:T(8,128)(2,1)} async-done(((bf16[8192,32]{0,1:T(8,128)(2,1)}), bf16[8192,256]{0,1:T(8,128)(2,1)}) %all-gather.2.cloned.1.call-update) | async-done | bytes 4194320 | tf_op jit(solution)/shard_map/all_gather | solution.py:43
  76.1 4.7 fusion.11
  80.9 0.1 copy.32
  81.1 11.7 %cholesky.50 = f32[128,128]{1,0:T(8,128)S(1)} custom-call(f32[128,128]{1,0:T(8,128)S(1)} %cholesky.118), custom_call_target="Cholesky" | custom-call | tf_op jit(solution)/shard_map/jit(cholesky)/cholesky | solution.py:77
  92.8 9.8 %custom-call.18 = f32[1,128,128]{1,2,0:T(8,128)S(1)} custom-call(f32[1,128,128]{2,1,0:T(8,128)S(1)} %get-tuple-element.274), custom_call_target="InvertDiagBlocksLowerTriangular" | custom-call | tf_op jit(solution)/shard_map/jit(cholesky)/cholesky | solution.py:77
  102.7 0.2 constant_dynamic-update-slice_fusion.1
  102.9 0.3 convolution_subtract_fusion.2
  103.1 11.7 %cholesky.105 = f32[128,128]{1,0:T(8,128)S(1)} custom-call(f32[128,128]{1,0:T(8,128)S(1)} %convolution_subtract_fusion.2), custom_call_target="Cholesky" | custom-call | tf_op jit(solution)/shard_map/jit(cholesky)/cholesky | solution.py:77
  114.8 6.4 %copy.34 = bf16[8192,256]{1,0:T(8,128)(2,1)} copy(bf16[8192,256]{0,1:T(8,128)(2,1)} %all-gather.2.cloned.1.call-done) | data formatting | bytes 8388608
  121.3 223.8 %while.15 = (s32[]{:T(128)}, f32[512,256]{1,0:T(8,128)S(1)}, s32[]{:T(128)}, s32[512]{0:T(512)}, s32[]{:T(128)}, /*index=5*/s32[512]{0:T(512)}, s32[]{:T(128)}, ...) while((s32[]{:T(128)}, f32[512,256]{1,0:T(8,128)S(1)}, ...), condition=%wide.region_7.8_spmd.clone, body=%wide.region_5.7_spmd.clone.sunk | while | flops 214271872 | bytes 27305452 | solution.py:75
  121.5 0.8 dynamic_slice.41
  122.2 0.7 add_compare_fusion.2
  122.9 0.9 fusion.42
  123.7 0.9 constant_dynamic-slice_fusion.5
  124.6 0.1 compare_select_fusion.4
  124.7 63.5 %gather_fusion = bf16[16384,256]{1,0:T(8,128)(2,1)} fusion(bf16[8192,256]{1,0:T(8,128)(2,1)} %get-tuple-element.438, s32[16384]{0:T(1024)S(1)} %broadcast_clamp_fusion.2), kind=kCustom, calls=%fused_computation.1.clone.clone.1 | custom fusion | bytes 16842752 | tf_op jit(solution)/shard_map/while/body/gather | solution.py:17
  188.2 5.5 %fusion.43 = f32[128,256]{1,0:T(8,128)S(1)} fusion(f32[128,128]{1,0:T(8,128)S(1)} %fusion.42, bf16[16384,256]{1,0:T(8,128)(2,1)} %gather_fusion), kind=kLoop, calls=%fused_computation.7.clone.1 | loop fusion | flops 12550144 | bytes 8585216 | tf_op jit(solution)/shard_map/while/body/reduce_sum | solution.py:19
  193.7 0.8 compare_select_fusion.5
  194.5 0.8 gather_fusion.1
  195.3 0.6 convolution_add_fusion.2
  196.0 0.8 dynamic_slice.41
  196.8 0.7 add_compare_fusion.2
  197.4 0.9 fusion.42
  198.3 0.9 constant_dynamic-slice_fusion.5
  199.2 63.5 %gather_fusion = bf16[16384,256]{1,0:T(8,128)(2,1)} fusion(bf16[8192,256]{1,0:T(8,128)(2,1)} %get-tuple-element.438, s32[16384]{0:T(1024)S(1)} %broadcast_clamp_fusion.2), kind=kCustom, calls=%fused_computation.1.clone.clone.1 | custom fusion | bytes 16842752 | tf_op jit(solution)/shard_map/while/body/gather | solution.py:17
  262.8 5.5 %fusion.43 = f32[128,256]{1,0:T(8,128)S(1)} fusion(f32[128,128]{1,0:T(8,128)S(1)} %fusion.42, bf16[16384,256]{1,0:T(8,128)(2,1)} %gather_fusion), kind=kLoop, calls=%fused_computation.7.clone.1 | loop fusion | flops 12550144 | bytes 8585216 | tf_op jit(solution)/shard_map/while/body/reduce_sum | solution.py:19
  268.2 0.8 compare_select_fusion.5
  269.0 0.8 gather_fusion.1
  269.9 0.6 convolution_add_fusion.2
  270.5 0.8 dynamic_slice.41
  271.3 0.7 add_compare_fusion.2
  271.9 0.9 fusion.42
  272.8 0.9 constant_dynamic-slice_fusion.5
  273.8 63.5 %gather_fusion = bf16[16384,256]{1,0:T(8,128)(2,1)} fusion(bf16[8192,256]{1,0:T(8,128)(2,1)} %get-tuple-element.438, s32[16384]{0:T(1024)S(1)} %broadcast_clamp_fusion.2), kind=kCustom, calls=%fused_computation.1.clone.clone.1 | custom fusion | bytes 16842752 | tf_op jit(solution)/shard_map/while/body/gather | solution.py:17
  337.3 5.5 %fusion.43 = f32[128,256]{1,0:T(8,128)S(1)} fusion(f32[128,128]{1,0:T(8,128)S(1)} %fusion.42, bf16[16384,256]{1,0:T(8,128)(2,1)} %gather_fusion), kind=kLoop, calls=%fused_computation.7.clone.1 | loop fusion | flops 12550144 | bytes 8585216 | tf_op jit(solution)/shard_map/while/body/reduce_sum | solution.py:19
  342.8 0.8 compare_select_fusion.5
  343.6 0.8 gather_fusion.1
  344.4 0.6 convolution_add_fusion.2
  345.1 1.0 copy.35
  346.1 0.7 compare_reduce_fusion
  348.1 0.1 triangular_solve.66
  348.2 3.9 while.14
  348.2 0.6 fusion.40
  348.8 1.3 bitcast_dynamic-update-slice_fusion.2
  350.1 0.6 fusion.40
  350.7 1.3 bitcast_dynamic-update-slice_fusion.2
  352.1 19.7 %custom-call.19 = f32[2,128,128]{1,2,0:T(8,128)S(1)} custom-call(f32[2,128,128]{2,1,0:T(8,128)S(1)} %get-tuple-element.189), custom_call_target="InvertDiagBlocksLowerTriangular" | custom-call | tf_op jit(solution)/shard_map/jit(_cho_solve)/triangular_solve | solution.py:78
  371.8 70.9 %reduce-scatter.2.cloned.1.call-done = f32[128,256]{0,1:T(8,128)} async-done(((f32[512,256]{0,1:T(8,128)}), f32[128,256]{0,1:T(8,128)}) %reduce-scatter.2.cloned.1.call-update) | async-done | bytes 131088 | tf_op jit(solution)/shard_map/reduce_scatter | solution.py:76
  442.6 1.1 fusion.13
  443.7 1.0 convolution_subtract_fusion.1
  444.8 0.3 fusion.20
  445.1 0.2 fusion.19
  445.3 0.3 convolution_subtract_fusion
  445.6 0.2 fusion.18
  445.8 11.8 %all_to_all.25 = f32[128,8,32]{0,2,1:T(8,128)S(1)} all-to-all(f32[128,8,32]{0,2,1:T(8,128)S(1)} %bitcast.67), channel_id=1, replica_groups=mesh['rows'=8,'cols'=4] {'rows'}, dimensions={1} | all-to-all | bytes 262144 | tf_op jit(solution)/shard_map/all_to_all | solution.py:80
  457.6 0.1 copy.36
  457.8 10.3 %all_to_all.26 = f32[4,256,32]{1,2,0:T(8,128)S(1)} all-to-all(f32[4,256,32]{1,2,0:T(8,128)S(1)} %copy.37), channel_id=1, replica_groups=mesh['rows'=8,'cols'=4] {'cols'}, dimensions={0} | all-to-all | bytes 262144 | tf_op jit(solution)/shard_map/all_to_all | solution.py:79
  468.2 0.1 copy.38
  468.3 0.7 reshape.103
  (29 shorter events, 0.7 us)
Async XLA Ops:
  7.4 50.3 %all-reduce.3.cloned.1.call-start = ((), (), s32[]{:S(2)}) async-start(), calls=%async_computation.3 | async-start | bytes 524288 | tf_op jit(solution)/shard_map/psum | solution.py:46
  20.1 56.0 %all-gather.2.cloned.1.call-start = ((), (), s32[]{:S(2)}) async-start(), calls=%async_computation.4 | async-start | bytes 4718592 | tf_op jit(solution)/shard_map/all_gather | solution.py:43
  41.0 401.6 %reduce-scatter.2.cloned.1.call-start = ((), (), s32[]{:S(2)}) async-start(), calls=%async_computation.5 | async-start | bytes 655360 | tf_op jit(solution)/shard_map/reduce_scatter | solution.py:76
Sparse Core Ops, SparseCore 0:
  20.2 37.4 all-reduce.2
  346.2 96.3 reduce-scatter.1
Sparse Core Ops, SparseCore 1:
  41.1 34.9 all-gather.1
where the time goes:
time: 478 us; the launch traced here: 476 us
  local copies, waits for them, and re-layouts  211 us (44%)
  waiting for transfers between devices  105 us (22%)
  other arithmetic  77.3 us (16%)
  blocking collectives  54.6 us (11%)
  between operations  17 us (4%)
  matrix products  11.3 us (2%)
    gather x3, local copies, waits for them, and re-layouts, block_fold(): picked = table[third.reshape(group * width)]  191 us
    reduce_scatter x1, waiting for transfers between devices, per_device(): lax.psum_scatter(partial_rows, 'cols', scatter_dimension=0, tiled=True)  70.9 us
    another operation x6, other arithmetic, per_device(): factor = jnp.linalg.cholesky(gram)  34 us
    all_gather x1, blocking collectives, per_device(): third_part = lax.all_gather(third_factor, 'cols', axis=0, tiled=True)  20.9 us
    another operation x4, other arithmetic, per_device(): solved = jax.scipy.linalg.cho_solve((factor, True), mine.T).T  19.7 us
    all_gather x1, waiting for transfers between devices, per_device(): third_whole = lax.all_gather(third_part, 'rows', axis=1, tiled=True)  18.4 us
    reduce_sum x3, other arithmetic, block_fold(): return jnp.sum(scaled.reshape(group, width, picked.shape[1]), axis=1)  16.4 us
    psum x1, waiting for transfers between devices, per_device(): gram_second = lax.psum(local_gram, 'cols') / (range_rows * n_cols)  15.7 us
  transfers between devices with their start and end apart: 3, of which 3 were waited for; matrix products, arithmetic and copies ran while one was open for 5% of the time, Pallas kernels for 0%

commit v1 on v0

--- a/solution.py
+++ b/solution.py
@@ -40,7 +40,8 @@
     owned = jnp.arange(slab, dtype=jnp.int32)
     second_range = lax.all_gather(second_factor, "rows", axis=1, tiled=True)
     third_part = lax.all_gather(third_factor, "cols", axis=0, tiled=True)
-    third_whole = lax.all_gather(third_part, "rows", axis=1, tiled=True)
+    stack = jnp.stack([third_part] * lax.axis_size("rows"))
+    third_whole = jnp.concatenate(lax.all_to_all(stack, "rows", 0, 0), axis=1)
     range_rows = second_range.shape[0]
     local_gram = gram_product(second_range, second_range)
     gram_second = lax.psum(local_gram, "cols") / (range_rows * n_cols)

time: 478 us -> 517 us (1.082)
  blocking collectives: 54.6 us -> 92.9 us
    all_gather x1, blocking collectives: 11.6 us -> 53.3 us  [per_device(): second_range = lax.all_gather(second_factor, 'rows', axis=1, tiled=True)]
    all_gather x1 -> x0, waiting for transfers between devices: 18.4 us -> none  [per_device(): third_whole = lax.all_gather(third_part, 'rows', axis=1, tiled=True)]
    psum x1, waiting for transfers between devices: 15.7 us -> 29.2 us  [per_device(): gram_second = lax.psum(local_gram, 'cols') / (range_rows * n_cols)]
  transfers between devices with their start and end apart: 3 -> 3, of which waited for: 3 -> 2; matrix products, arithmetic and copies ran while one was open for 5% -> 6% of each run, Pallas kernels for 0% -> 0%
where the time goes in v1:
time: 517 us; the launch traced here: 515 us
  local copies, waits for them, and re-layouts  213 us (41%)
  waiting for transfers between devices  100 us (19%)
  blocking collectives  92.9 us (18%)
  other arithmetic  77.4 us (15%)
  between operations  15.6 us (3%)
  matrix products  11.3 us (2%)
    gather x3, local copies, waits for them, and re-layouts, block_fold(): picked = table[third.reshape(group * width)]  190 us
    reduce_scatter x1, waiting for transfers between devices, per_device(): lax.psum_scatter(partial_rows, 'cols', scatter_dimension=0, tiled=True)  70.7 us
    all_gather x1, blocking collectives, per_device(): second_range = lax.all_gather(second_factor, 'rows', axis=1, tiled=True)  53.3 us
    another operation x6, other arithmetic, per_device(): factor = jnp.linalg.cholesky(gram)  34 us
    psum x1, waiting for transfers between devices, per_device(): gram_second = lax.psum(local_gram, 'cols') / (range_rows * n_cols)  29.2 us
    another operation x4, other arithmetic, per_device(): solved = jax.scipy.linalg.cho_solve((factor, True), mine.T).T  19.7 us
    all_gather x1, blocking collectives, per_device(): third_part = lax.all_gather(third_factor, 'cols', axis=0, tiled=True)  17.6 us
    reduce_sum x3, other arithmetic, block_fold(): return jnp.sum(scaled.reshape(group, width, picked.shape[1]), axis=1)  16.5 us
  transfers between devices with their start and end apart: 3, of which 2 were waited for; matrix products, arithmetic and copies ran while one was open for 6% of the time, Pallas kernels for 0%

profile of v1, /device:TPU:0, one launch (start us, length us, event | category | flops | bytes accessed | tf_op | source)
XLA Modules:
  0.0 515.3 jit_solution(12662290807586055291)
XLA Ops:
  6.5 17.6 %all_gather.7 = bf16[8192,32]{0,1:T(8,128)(2,1)S(1)} all-gather(bf16[2048,32]{0,1:T(8,128)(2,1)} %param.17), channel_id=1, replica_groups=mesh['rows'=8,'cols'=4] {'cols'}, dimensions={0}, use_global_device_ids=true | all-gather | bytes 655360 | tf_op jit(solution)/shard_map/all_gather | solution.py:42
  24.1 2.4 stack.2
  26.5 4.7 all-to-all-start
  31.3 53.3 %all_gather.6 = bf16[1024,256]{0,1:T(8,128)(2,1)S(1)} all-gather(bf16[1024,32]{0,1:T(8,128)(2,1)S(1)} %copy-done), channel_id=1, replica_groups=mesh['rows'=8,'cols'=4] {'rows'}, dimensions={1}, use_global_device_ids=true | all-gather | bytes 589824 | tf_op jit(solution)/shard_map/all_gather | solution.py:41
  84.6 1.0 fusion.24
  86.4 0.2 copy.33
  86.7 6.4 %copy.34 = bf16[8192,256]{1,0:T(8,128)(2,1)} copy(bf16[8192,256]{0,1:T(8,128)(2,1)} %bitcast.1) | data formatting | bytes 8388608
  93.0 29.2 %all-reduce.3.cloned.1.call-done = f32[256,256]{0,1:T(8,128)} async-done(((f32[256,256]{0,1:T(8,128)}), f32[256,256]{0,1:T(8,128)}) %all-reduce.3.cloned.1.call-update) | async-done | bytes 262160 | tf_op jit(solution)/shard_map/psum | solution.py:47
  122.2 4.7 fusion.11
  127.0 0.1 copy.32
  127.2 11.7 %cholesky.50 = f32[128,128]{1,0:T(8,128)S(1)} custom-call(f32[128,128]{1,0:T(8,128)S(1)} %cholesky.118), custom_call_target="Cholesky" | custom-call | tf_op jit(solution)/shard_map/jit(cholesky)/cholesky | solution.py:78
  138.9 9.8 %custom-call.18 = f32[1,128,128]{1,2,0:T(8,128)S(1)} custom-call(f32[1,128,128]{2,1,0:T(8,128)S(1)} %get-tuple-element.300), custom_call_target="InvertDiagBlocksLowerTriangular" | custom-call | tf_op jit(solution)/shard_map/jit(cholesky)/cholesky | solution.py:78
  148.8 0.2 constant_dynamic-update-slice_fusion.1
  149.0 0.3 convolution_subtract_fusion.2
  149.2 11.7 %cholesky.105 = f32[128,128]{1,0:T(8,128)S(1)} custom-call(f32[128,128]{1,0:T(8,128)S(1)} %convolution_subtract_fusion.2), custom_call_target="Cholesky" | custom-call | tf_op jit(solution)/shard_map/jit(cholesky)/cholesky | solution.py:78
  161.0 223.7 %while.15 = (s32[]{:T(128)}, f32[512,256]{1,0:T(8,128)S(1)}, s32[]{:T(128)}, s32[512]{0:T(512)}, s32[]{:T(128)}, /*index=5*/s32[512]{0:T(512)}, s32[]{:T(128)}, ...) while((s32[]{:T(128)}, f32[512,256]{1,0:T(8,128)S(1)}, ...), condition=%wide.region_7.8_spmd.clone, body=%wide.region_5.7_spmd.clone.sunk | while | flops 214271872 | bytes 27305452 | solution.py:76
  161.2 0.8 dynamic_slice.41
  162.0 0.7 add_compare_fusion.2
  162.6 0.9 fusion.42
  163.5 0.9 constant_dynamic-slice_fusion.5
  164.4 63.5 %gather_fusion = bf16[16384,256]{1,0:T(8,128)(2,1)} fusion(bf16[8192,256]{1,0:T(8,128)(2,1)} %get-tuple-element.464, s32[16384]{0:T(1024)S(1)} %broadcast_clamp_fusion.2), kind=kCustom, calls=%fused_computation.1.clone.clone.1 | custom fusion | bytes 16842752 | tf_op jit(solution)/shard_map/while/body/gather | solution.py:17
  227.9 5.5 %fusion.43 = f32[128,256]{1,0:T(8,128)S(1)} fusion(f32[128,128]{1,0:T(8,128)S(1)} %fusion.42, bf16[16384,256]{1,0:T(8,128)(2,1)} %gather_fusion), kind=kLoop, calls=%fused_computation.7.clone.1 | loop fusion | flops 12550144 | bytes 8585216 | tf_op jit(solution)/shard_map/while/body/reduce_sum | solution.py:19
  233.4 0.8 compare_select_fusion.5
  234.2 0.8 gather_fusion.1
  235.0 0.6 convolution_add_fusion.2
  235.7 0.8 dynamic_slice.41
  236.5 0.7 add_compare_fusion.2
  237.1 0.9 fusion.42
  238.0 0.9 constant_dynamic-slice_fusion.5
  238.9 63.5 %gather_fusion = bf16[16384,256]{1,0:T(8,128)(2,1)} fusion(bf16[8192,256]{1,0:T(8,128)(2,1)} %get-tuple-element.464, s32[16384]{0:T(1024)S(1)} %broadcast_clamp_fusion.2), kind=kCustom, calls=%fused_computation.1.clone.clone.1 | custom fusion | bytes 16842752 | tf_op jit(solution)/shard_map/while/body/gather | solution.py:17
  302.4 5.5 %fusion.43 = f32[128,256]{1,0:T(8,128)S(1)} fusion(f32[128,128]{1,0:T(8,128)S(1)} %fusion.42, bf16[16384,256]{1,0:T(8,128)(2,1)} %gather_fusion), kind=kLoop, calls=%fused_computation.7.clone.1 | loop fusion | flops 12550144 | bytes 8585216 | tf_op jit(solution)/shard_map/while/body/reduce_sum | solution.py:19
  307.9 0.8 compare_select_fusion.5
  308.7 0.8 gather_fusion.1
  309.5 0.6 convolution_add_fusion.2
  310.2 0.8 dynamic_slice.41
  311.0 0.7 add_compare_fusion.2
  311.6 0.9 fusion.42
  312.5 0.9 constant_dynamic-slice_fusion.5
  313.4 63.5 %gather_fusion = bf16[16384,256]{1,0:T(8,128)(2,1)} fusion(bf16[8192,256]{1,0:T(8,128)(2,1)} %get-tuple-element.464, s32[16384]{0:T(1024)S(1)} %broadcast_clamp_fusion.2), kind=kCustom, calls=%fused_computation.1.clone.clone.1 | custom fusion | bytes 16842752 | tf_op jit(solution)/shard_map/while/body/gather | solution.py:17
  376.9 5.5 %fusion.43 = f32[128,256]{1,0:T(8,128)S(1)} fusion(f32[128,128]{1,0:T(8,128)S(1)} %fusion.42, bf16[16384,256]{1,0:T(8,128)(2,1)} %gather_fusion), kind=kLoop, calls=%fused_computation.7.clone.1 | loop fusion | flops 12550144 | bytes 8585216 | tf_op jit(solution)/shard_map/while/body/reduce_sum | solution.py:19
  382.4 0.8 compare_select_fusion.5
  383.2 0.8 gather_fusion.1
  384.0 0.6 convolution_add_fusion.2
  384.7 1.0 copy.35
  385.7 0.7 compare_reduce_fusion
  387.7 0.1 triangular_solve.66
  387.8 3.9 while.14
  387.8 0.6 fusion.40
  388.4 1.3 bitcast_dynamic-update-slice_fusion.2
  389.8 0.6 fusion.40
  390.3 1.3 bitcast_dynamic-update-slice_fusion.2
  391.7 19.7 %custom-call.19 = f32[2,128,128]{1,2,0:T(8,128)S(1)} custom-call(f32[2,128,128]{2,1,0:T(8,128)S(1)} %get-tuple-element.189), custom_call_target="InvertDiagBlocksLowerTriangular" | custom-call | tf_op jit(solution)/shard_map/jit(_cho_solve)/triangular_solve | solution.py:79
  411.4 70.7 %reduce-scatter.2.cloned.1.call-done = f32[128,256]{0,1:T(8,128)} async-done(((f32[512,256]{0,1:T(8,128)}), f32[128,256]{0,1:T(8,128)}) %reduce-scatter.2.cloned.1.call-update) | async-done | bytes 131088 | tf_op jit(solution)/shard_map/reduce_scatter | solution.py:77
  482.1 1.1 fusion.13
  483.3 1.0 convolution_subtract_fusion.1
  484.3 0.3 fusion.20
  484.6 0.2 fusion.19
  484.8 0.3 convolution_subtract_fusion
  485.1 0.2 fusion.18
  485.3 11.8 %all_to_all.30 = f32[128,8,32]{0,2,1:T(8,128)S(1)} all-to-all(f32[128,8,32]{0,2,1:T(8,128)S(1)} %bitcast.70), channel_id=1, replica_groups=mesh['rows'=8,'cols'=4] {'rows'}, dimensions={1} | all-to-all | bytes 262144 | tf_op jit(solution)/shard_map/all_to_all | solution.py:81
  497.2 0.1 copy.36
  497.3 10.2 %all_to_all.31 = f32[4,256,32]{1,2,0:T(8,128)S(1)} all-to-all(f32[4,256,32]{1,2,0:T(8,128)S(1)} %copy.37), channel_id=1, replica_groups=mesh['rows'=8,'cols'=4] {'cols'}, dimensions={0} | all-to-all | bytes 262144 | tf_op jit(solution)/shard_map/all_to_all | solution.py:80
  507.6 0.1 copy.38
  507.7 0.7 reshape.113
  (31 shorter events, 0.8 us)
Async XLA Ops:
  26.5 4.8 copy-start
  26.5 60.1 %all-to-all-start = ((bf16[8,8192,32]{1,2,0:T(8,128)(2,1)}), bf16[8,8192,32]{1,2,0:T(8,128)(2,1)}, u32[]{:S(2)}, u32[]{:S(2)}) async-start(bf16[8,8192,32]{1,2,0:T(8,128)(2,1)} %stack.2), calls=%async_computation | async-start | bytes 8388608 | tf_op jit(solution)/shard_map/all_to_all | solution.py:44
  31.2 91.0 %all-reduce.3.cloned.1.call-start = ((), (), s32[]{:S(2)}) async-start(), calls=%async_computation.4 | async-start | bytes 524288 | tf_op jit(solution)/shard_map/psum | solution.py:47
  85.7 396.4 %reduce-scatter.2.cloned.1.call-start = ((), (), s32[]{:S(2)}) async-start(), calls=%async_computation.5 | async-start | bytes 655360 | tf_op jit(solution)/shard_map/reduce_scatter | solution.py:77
Sparse Core Ops, SparseCore 0:
  85.8 36.3 all-reduce.2
  385.8 96.2 reduce-scatter.1
